TPU v7x, 256 devices: a whole 4x4x8 slice. The times are simulated.
256 devices in a mesh: dp: 32 (over y, z), vocab: 8 (over x, core).
Axes of the slice: x: 4, y: 4, z: 8, core: 2. Of those that a mesh axis runs over, the one named last changes fastest.
Arguments:
- hidden: bfloat16 [24576, 2048], P('dp', 'vocab')
- gain: bfloat16 [2048], replicated, may hold values from 0.5 to 1.5
- head: bfloat16 [2048, 32000], P('dp', 'vocab')
- target_ids: int32 [24576], P('dp'), may hold values from 0 to 31999
- seq_lens: int32 [64], replicated, may hold values from 64 to 704, as said below
- seq_owner: int32 [64], replicated, may hold values from 0 to 31, as said below
Outputs:
- logprob: float32 [24576], P('dp')
- entropy: float32 [24576], P('dp')
Inputs may be any that keep to these rules, and one draw needn't show every extreme that they name: `seq_lens`: the lengths of the sequences owned by one dp index sum to at most 768; in every draw the sequences of some dp index sum to exactly 768. `seq_owner`: every dp index owns exactly 2 sequences.
All inputs are finite; a program needn't handle non-finite values.
Results may differ from a plain program's by a relative error of at most 0.0075.
Values may be sent and summed in bfloat16 or wider, within the bound.
A program may use at most 64 MiB of HBM per device.

v0:
```python
import jax
import jax.numpy as jnp
from jax import lax
from jax.sharding import PartitionSpec as P

EPS = 1e-05


def chunk_bounds(breadth, parts):
    step = -(-breadth // parts)
    step = -(-step // 128) * 128
    bounds = []
    start = 0
    while start < breadth:
        stop = min(start + step, breadth)
        bounds.append((start, stop))
        start = stop
    return bounds


def chunk_stats(normed, columns, local_id, start):
    logits = jnp.dot(normed, columns, preferred_element_type=jnp.float32)
    top = jnp.max(logits, axis=1)
    expo = jnp.exp(logits - top[:, None])
    total = jnp.sum(expo, axis=1)
    weighted = jnp.sum(expo * logits, axis=1)
    ids = start + lax.broadcasted_iota(jnp.int32, logits.shape, 1)
    picked = jnp.sum(jnp.where(ids == local_id[:, None], logits, 0.0), axis=1)
    return (top, total, weighted, picked)


def local(hidden, gain, head, target_ids, seq_lens, seq_owner):
    groups = lax.axis_size("dp")
    position = lax.axis_index("dp")
    slice_index = lax.axis_index("vocab")
    slots = hidden.shape[0]
    breadth = head.shape[1]
    owners = jnp.arange(groups, dtype=jnp.int32)
    loads = jnp.sum(jnp.where(seq_owner[:, None] == owners[None, :], seq_lens[:, None], 0), axis=0)
    own_live = jnp.arange(slots, dtype=jnp.int32) < loads[position]
    features = lax.all_gather(hidden, "vocab", axis=1, tiled=True)
    wide = features.astype(jnp.float32)
    normed = (
        wide
        * lax.rsqrt(jnp.mean(wide * wide, axis=1, keepdims=True) + EPS)
        * gain.astype(jnp.float32)
    ).astype(jnp.bfloat16)
    local_id = target_ids - slice_index * breadth
    parts = []
    for start, stop in chunk_bounds(breadth, 4):
        columns = lax.all_gather(head[:, start:stop], "dp", axis=0, tiled=True)
        parts.append(chunk_stats(normed, columns, local_id, start))
    tops = jnp.stack([p[0] for p in parts])
    top_local = jnp.max(tops, axis=0)
    scale = jnp.exp(tops - top_local[None, :])
    total_local = jnp.sum(jnp.stack([p[1] for p in parts]) * scale, axis=0)
    weighted_local = jnp.sum(jnp.stack([p[2] for p in parts]) * scale, axis=0)
    picked_local = jnp.sum(jnp.stack([p[3] for p in parts]), axis=0)
    top = lax.pmax(top_local, "vocab")
    factor = jnp.exp(top_local - top)
    total, weighted, picked = lax.psum(
        (total_local * factor, weighted_local * factor, picked_local), "vocab"
    )
    lse = top + jnp.log(total)
    logprob = picked - lse
    entropy = lse - weighted / total
    return (jnp.where(own_live, logprob, 0.0), jnp.where(own_live, entropy, 0.0))


def solution(mesh):
    return jax.shard_map(
        local,
        mesh=mesh,
        in_specs=(P("dp", "vocab"), P(), P("dp", "vocab"), P("dp"), P(), P()),
        out_specs=(P("dp"), P("dp")),
        check_vma=False,
    )
```

profile of v0, /device:TPU:32, one launch (start us, length us, event | category | flops | bytes accessed | tf_op | source)
XLA Modules:
  0.0 432.0 jit_solution(7421292452426967437)
XLA Ops:
  7.2 0.0 all-gather.6.cloned.1.call-start
  7.2 0.7 all-gather.6.cloned.1.call-update
  7.9 0.0 all-gather.14.cloned.1.call-start
  7.9 1.6 slice.15
  9.5 0.0 all-gather.14.cloned.1.call-update
  9.5 0.0 all-gather.8.cloned.1.call-start
  9.6 1.8 fusion.20
  11.4 0.0 all-gather.8.cloned.1.call-update
  11.4 0.0 all-gather.10.cloned.1.call-start
  11.5 0.5 all-gather.10.cloned.1.call-update
  12.0 0.0 all-gather.12.cloned.1.call-start
  12.0 0.5 all-gather.12.cloned.1.call-update
  12.6 0.7 convert_element_type.10
  13.3 0.8 select_reduce_fusion.4
  14.1 0.7 dynamic_slice.3
  14.7 0.7 broadcast_subtract_fusion
  15.4 31.2 %all-gather.6.cloned.1.call-done = bf16[768,2048]{1,0:T(8,128)(2,1)} async-done(((bf16[768,256]{1,0:T(8,128)(2,1)}), bf16[768,2048]{1,0:T(8,128)(2,1)}) %all-gather.6.cloned.1.call-update) | async-done | bytes 3145744 | tf_op jit(solution)/shard_map/all_gather | solution.py:41
  46.6 0.0 copy-start.1
  46.6 2.7 fusion
  49.4 82.9 %all-gather.14.cloned.1.call-done = bf16[2048,928]{1,0:T(8,128)(2,1)} async-done(((bf16[64,928]{1,0:T(8,128)(2,1)}), bf16[2048,928]{1,0:T(8,128)(2,1)}) %all-gather.14.cloned.1.call-update) | async-done | bytes 3801104 | tf_op jit(solution)/shard_map/all_gather | solution.py:51
  132.3 0.0 copy-done.1
  132.3 5.9 %fusion.21 = (f32[768]{0:T(1024)S(1)}, f32[768,928]{0,1:T(8,128)S(1)}) fusion(bf16[2048,928]{1,0:T(8,128)(2,1)} %all-gather.14.cloned.1.call-done, bf16[768,2048]{1,0:T(8,128)(2,1)S(1)} %copy-done.1, f32[2048]{0:T(1024)S(1)} %convert_element_type.10, f32[768]{0:T(1024)S(1)} %add_rsqrt_fusion), kind=kOutput, calls=%fused_computation.49 | convolution fusion | flops 2926238976 | bytes 9811968 | tf_op jit(solution)/shard_map/dot_general | solution.py:22
  138.2 0.9 multiply_reduce_fusion.3
  139.0 74.9 %all-gather.8.cloned.1.call-done = bf16[2048,1024]{1,0:T(8,128)(2,1)} async-done(((bf16[64,1024]{1,0:T(8,128)(2,1)}), bf16[2048,1024]{1,0:T(8,128)(2,1)}) %all-gather.8.cloned.1.call-update) | async-done | bytes 4194320 | tf_op jit(solution)/shard_map/all_gather | solution.py:51
  214.0 6.4 %fusion.24 = (f32[768]{0:T(1024)S(1)}, f32[768,1024]{1,0:T(8,128)S(1)}) fusion(bf16[2048,1024]{1,0:T(8,128)(2,1)} %all-gather.8.cloned.1.call-done, bf16[768,2048]{1,0:T(8,128)(2,1)} %all-gather.6.cloned.1.call-done, f32[2048]{0:T(1024)S(1)} %convert_element_type.10, f32[768]{0:T(1024)S(1)} %add_rsqrt_fusion), kind=kOutput, calls=%fused_computation.52 | convolution fusion | flops 3228302592 | bytes 10500096 | tf_op jit(solution)/shard_map/dot_general | solution.py:22
  220.4 75.1 %all-gather.10.cloned.1.call-done = bf16[2048,1024]{1,0:T(8,128)(2,1)} async-done(((bf16[64,1024]{1,0:T(8,128)(2,1)}), bf16[2048,1024]{1,0:T(8,128)(2,1)}) %all-gather.10.cloned.1.call-update) | async-done | bytes 4194320 | tf_op jit(solution)/shard_map/all_gather | solution.py:51
  295.5 8.4 %fusion.22 = (f32[768]{0:T(1024)S(1)}, f32[768,1024]{1,0:T(8,128)}) fusion(bf16[2048,1024]{1,0:T(8,128)(2,1)} %all-gather.10.cloned.1.call-done, bf16[768,2048]{1,0:T(8,128)(2,1)} %all-gather.6.cloned.1.call-done, f32[2048]{0:T(1024)S(1)} %convert_element_type.10, f32[768]{0:T(1024)S(1)} %add_rsqrt_fusion), kind=kOutput, calls=%fused_computation.50 | convolution fusion | flops 3228302592 | bytes 10500096 | tf_op jit(solution)/shard_map/dot_general | solution.py:22
  303.8 73.2 %all-gather.12.cloned.1.call-done = bf16[2048,1024]{1,0:T(8,128)(2,1)} async-done(((bf16[64,1024]{1,0:T(8,128)(2,1)}), bf16[2048,1024]{1,0:T(8,128)(2,1)}) %all-gather.12.cloned.1.call-update) | async-done | bytes 4194320 | tf_op jit(solution)/shard_map/all_gather | solution.py:51
  377.0 0.0 copy-start
  377.0 6.6 %fusion.23 = (f32[768]{0:T(1024)S(1)}, f32[768,1024]{1,0:T(8,128)S(1)}) fusion(bf16[2048,1024]{1,0:T(8,128)(2,1)} %all-gather.12.cloned.1.call-done, bf16[768,2048]{1,0:T(8,128)(2,1)} %all-gather.6.cloned.1.call-done, f32[2048]{0:T(1024)S(1)} %convert_element_type.10, f32[768]{0:T(1024)S(1)} %add_rsqrt_fusion), kind=kOutput, calls=%fused_computation.51 | convolution fusion | flops 3228302592 | bytes 10500096 | tf_op jit(solution)/shard_map/dot_general | solution.py:22
  383.6 0.0 copy-done
  383.6 4.4 %multiply_reduce_fusion.1 = (f32[768]{0:T(1024)S(1)}, f32[768]{0:T(1024)S(1)}, f32[768]{0:T(1024)S(1)}, f32[768]{0:T(1024)S(1)}, f32[768]{0:T(1024)S(1)}, /*inde...) fusion(f32[768,1024]{1,0:T(8,128)S(1)} %copy-done, f32[768]{0:T(1024)S(1)} %get-tuple-element.34, ...), kind=kLoop, calls=%fused_computation.6 | loop fusion | flops 16508160 | bytes 9485312 | tf_op jit(solution)/shard_map/reduce_sum | solution.py:26
  388.1 12.4 %pmax.7 = f32[768]{0:T(1024)S(1)} all-reduce(f32[768]{0:T(1024)S(1)} %maximum_maximum_fusion), channel_id=1, replica_groups=mesh['dp'=32,'vocab'=8] {'vocab'}, use_global_device_ids=true, to_apply=%region_11.12 | all-reduce | flops 768 | bytes 6144 | tf_op jit(solution)/shard_map/pmax | solution.py:59
  400.5 0.1 fusion.9
  400.6 23.6 %all-reduce = (f32[768]{0:T(1024)S(1)}, f32[768]{0:T(1024)S(1)}, f32[768]{0:T(1024)S(1)}) all-reduce(f32[768]{0:T(1024)S(1)} %add_add_fusion, f32[768]{0:T(1024)S(1)} %get-tuple-element.25, f32[768]{0:T(1024)S(1)} %get-tuple-element.24), channel_id=1, replica_groups=mesh['dp'=32,'vocab'=8] {'vocab'}, use_global_device_ids=true, to_apply=%region_6.7 | all-reduce | flops 2304 | bytes 18432 | tf_op jit(solution)/shard_map/psum | solution.py:61
  424.2 1.3 subtract_select_fusion
  (18 shorter events, 0.1 us)
Async XLA Ops:
  7.2 39.5 %all-gather.6.cloned.1.call-start = ((), (), s32[]{:S(2)}) async-start(), calls=%async_computation | async-start | bytes 3538944 | tf_op jit(solution)/shard_map/all_gather | solution.py:41
  7.9 124.4 %all-gather.14.cloned.1.call-start = ((), (), s32[]{:S(2)}) async-start(), calls=%async_computation.4 | async-start | bytes 4325376 | tf_op jit(solution)/shard_map/all_gather | solution.py:51
  9.5 204.4 %all-gather.8.cloned.1.call-start = ((), (), s32[]{:S(2)}) async-start(), calls=%async_computation.1 | async-start | bytes 4325376 | tf_op jit(solution)/shard_map/all_gather | solution.py:51
  11.4 284.1 %all-gather.10.cloned.1.call-start = ((), (), s32[]{:S(2)}) async-start(), calls=%async_computation.2 | async-start | bytes 4325376 | tf_op jit(solution)/shard_map/all_gather | solution.py:51
  12.0 365.0 %all-gather.12.cloned.1.call-start = ((), (), s32[]{:S(2)}) async-start(), calls=%async_computation.3 | async-start | bytes 4325376 | tf_op jit(solution)/shard_map/all_gather | solution.py:51
  46.6 85.6 %copy-start.1 = (bf16[768,2048]{1,0:T(8,128)(2,1)S(1)}, bf16[768,2048]{1,0:T(8,128)(2,1)}, u32[]{:S(2)}) copy-start(bf16[768,2048]{1,0:T(8,128)(2,1)} %all-gather.6.cloned.1.call-done) | copy-start | bytes 9437188
  377.0 6.6 %copy-start = (f32[768,1024]{1,0:T(8,128)S(1)}, f32[768,1024]{1,0:T(8,128)}, u32[]{:S(2)}) copy-start(f32[768,1024]{1,0:T(8,128)} %get-tuple-element.35) | copy-start | bytes 9437188
Sparse Core Ops, SparseCore 0:
  9.8 36.7 all-gather.5
  49.2 83.0 all-gather.13
  134.9 79.0 all-gather.7
  216.4 79.0 all-gather.9
  297.9 79.0 all-gather.11
where the time goes:
time: 432 us
  waiting for transfers between devices  339 us (78%)
  blocking collectives  36 us (8%)
  matrix products  27.2 us (6%)
  between operations  13.9 us (3%)
  other arithmetic  11.6 us (3%)
    all_gather x4, waiting for transfers between devices, local(): columns = lax.all_gather(head[:, start:stop], 'dp', axis=0, tiled=True)  306 us
    all_gather x1, waiting for transfers between devices, local(): features = lax.all_gather(hidden, 'vocab', axis=1, tiled=True)  31.2 us
    dot_general x4, matrix products, chunk_stats(): logits = jnp.dot(normed, columns, preferred_element_type=jnp.float32)  27.2 us
    psum x1, blocking collectives, local(): lax.psum((total_local * factor, weighted_local * factor, picked_local), '...  23.6 us
    pmax x1, blocking collectives, local(): top = lax.pmax(top_local, 'vocab')  12.4 us
  transfers between devices with their start and end apart: 5, of which 5 were waited for; matrix products, arithmetic and copies ran while one was open for 7% of the time, Pallas kernels for 0%

commit v1 on v0

--- a/solution.py
+++ b/solution.py
@@ -48,7 +48,9 @@
     local_id = target_ids - slice_index * breadth
     parts = []
     for start, stop in chunk_bounds(breadth, 4):
-        columns = lax.all_gather(head[:, start:stop], "dp", axis=0, tiled=True)
+        x = head[:, start:stop]
+        copies = jnp.concatenate([x] * lax.axis_size("dp"), axis=0)
+        columns = lax.all_to_all(copies, "dp", 0, 0, tiled=True)
         parts.append(chunk_stats(normed, columns, local_id, start))
     tops = jnp.stack([p[0] for p in parts])
     top_local = jnp.max(tops, axis=0)

time: 432 us -> 494 us (1.14)
  local copies, waits for them, and re-layouts: 4.11 us -> 78.8 us
  waiting for transfers between devices: 339 us -> 292 us
  starting transfers between devices: 0.2 us -> 32.3 us
    all_gather x4 -> x0, waiting for transfers between devices: 306 us -> none  [local(): columns = lax.all_gather(head[:, start:stop], 'dp', axis=0, tiled=True)]
    all_to_all x0 -> x4, waiting for transfers between devices: none -> 291 us  [local(): columns = lax.all_to_all(copies, 'dp', 0, 0, tiled=True)]
    unnamed x4 -> x139, local copies, waits for them, and re-layouts: 0.01 us -> 76 us
    all_to_all x0 -> x4, starting transfers between devices: none -> 32.3 us  [local(): columns = lax.all_to_all(copies, 'dp', 0, 0, tiled=True)]
    all_gather x1, waiting for transfers between devices: 31.2 us -> 0.02 us  [local(): features = lax.all_gather(hidden, 'vocab', axis=1, tiled=True)]
  transfers between devices with their start and end apart: 5 -> 5, of which waited for: 5 -> 4; matrix products, arithmetic and copies ran while one was open for 7% -> 18% of each run, Pallas kernels for 0% -> 0%
where the time goes in v1:
time: 494 us; the launch traced here: 493 us
  waiting for transfers between devices  292 us (59%)
  local copies, waits for them, and re-layouts  78.8 us (16%)
  blocking collectives  38.3 us (8%)
  starting transfers between devices  32.3 us (7%)
  matrix products  28.1 us (6%)
  between operations  14.5 us (3%)
  other arithmetic  9.21 us (2%)
    all_to_all x4, waiting for transfers between devices, local(): columns = lax.all_to_all(copies, 'dp', 0, 0, tiled=True)  291 us
    unnamed x139, local copies, waits for them, and re-layouts  76 us
    all_to_all x4, starting transfers between devices, local(): columns = lax.all_to_all(copies, 'dp', 0, 0, tiled=True)  32.3 us
    dot_general x4, matrix products, chunk_stats(): logits = jnp.dot(normed, columns, preferred_element_type=jnp.float32)  28.1 us
    psum x1, blocking collectives, local(): lax.psum((total_local * factor, weighted_local * factor, picked_local), '...  23.6 us
    pmax x1, blocking collectives, local(): top = lax.pmax(top_local, 'vocab')  14.7 us
  transfers between devices with their start and end apart: 5, of which 4 were waited for; matrix products, arithmetic and copies ran while one was open for 18% of the time, Pallas kernels for 0%

profile of v1, /device:TPU:32, one launch (start us, length us, event | category | flops | bytes accessed | tf_op | source)
XLA Modules:
  0.0 493.5 jit_solution(12105957242149085369)
XLA Ops:
  7.2 1.0 constant_dynamic-update-slice_fusion.127
  8.2 0.9 constant_dynamic-update-slice_fusion.126
  9.1 0.9 constant_dynamic-update-slice_fusion.125
  10.0 0.9 constant_dynamic-update-slice_fusion.124
  10.9 0.9 constant_dynamic-update-slice_fusion.123
  11.8 0.9 constant_dynamic-update-slice_fusion.122
  12.8 0.9 constant_dynamic-update-slice_fusion.121
  13.7 0.9 constant_dynamic-update-slice_fusion.120
  14.6 0.9 constant_dynamic-update-slice_fusion.119
  15.5 0.9 constant_dynamic-update-slice_fusion.118
  16.4 0.9 constant_dynamic-update-slice_fusion.117
  17.4 0.9 constant_dynamic-update-slice_fusion.116
  18.3 0.9 constant_dynamic-update-slice_fusion.115
  19.2 0.9 constant_dynamic-update-slice_fusion.114
  20.1 0.9 constant_dynamic-update-slice_fusion.113
  21.0 0.9 constant_dynamic-update-slice_fusion.112
  22.3 2.0 copy-done.1
  24.2 11.4 %all-to-all-start.3 = ((bf16[32,64,928]{2,1,0:T(8,128)(2,1)}), bf16[32,64,928]{2,1,0:T(8,128)(2,1)}, u32[]{:S(2)}, u32[]{:S(2)}) async-start(bf16[32,64,928]{2,1,0:T(8,128)(2,1)} %bitcast.14), calls=%async_computation.3 | async-start | bytes 8388608 | tf_op jit(solution)/shard_map/all_to_all | solution.py:53
  35.7 0.7 constant_dynamic-update-slice_fusion.63
  38.3 0.7 constant_dynamic-update-slice_fusion.59
  38.9 0.7 constant_dynamic-update-slice_fusion.58
  40.9 0.7 constant_dynamic-update-slice_fusion.55
  41.6 0.7 constant_dynamic-update-slice_fusion.54
  45.5 0.7 constant_dynamic-update-slice_fusion.48
  48.1 0.7 constant_dynamic-update-slice_fusion.44
  49.5 0.7 constant_dynamic-update-slice_fusion.42
  52.8 0.7 constant_dynamic-update-slice_fusion.37
  56.0 0.8 constant_dynamic-update-slice_fusion.32
  56.8 0.7 constant_dynamic-update-slice_fusion.30
  57.4 0.7 constant_dynamic-update-slice_fusion.29
  58.8 0.7 constant_dynamic-update-slice_fusion.27
  60.8 0.7 constant_dynamic-update-slice_fusion.24
  62.1 0.7 constant_dynamic-update-slice_fusion.22
  63.4 0.7 constant_dynamic-update-slice_fusion.20
  66.0 0.7 constant_dynamic-update-slice_fusion.16
  68.6 0.7 constant_dynamic-update-slice_fusion.12
  73.3 57.9 %all-to-all-done.3 = bf16[32,64,928]{2,1,0:T(8,128)(2,1)} async-done(((bf16[32,64,928]{2,1,0:T(8,128)(2,1)}), bf16[32,64,928]{2,1,0:T(8,128)(2,1)}, u32[]{:S(2)}, u32[]{:S(2)}) %all-to-all-start.3) | async-done | bytes 3801120 | tf_op jit(solution)/shard_map/all_to_all | solution.py:53
  131.2 6.7 %all-to-all-start.1 = ((bf16[32,64,1024]{2,1,0:T(8,128)(2,1)}), bf16[32,64,1024]{2,1,0:T(8,128)(2,1)}, u32[]{:S(2)}, u32[]{:S(2)}) async-start(bf16[32,64,1024]{2,1,0:T(8,128)(2,1)} %bitcast.3), calls=%async_computation.1 | async-start | bytes 8388608 | tf_op jit(solution)/shard_map/all_to_all | solution.py:53
  141.2 0.7 constant_dynamic-update-slice_fusion
  143.2 0.7 constant_dynamic-update-slice_fusion.91
  143.9 0.7 constant_dynamic-update-slice_fusion.90
  144.5 0.7 constant_dynamic-update-slice_fusion.89
  145.2 0.7 constant_dynamic-update-slice_fusion.88
  150.5 0.7 constant_dynamic-update-slice_fusion.80
  153.1 0.7 constant_dynamic-update-slice_fusion.76
  153.8 0.7 constant_dynamic-update-slice_fusion.75
  154.4 0.7 constant_dynamic-update-slice_fusion.74
  161.0 0.7 constant_dynamic-update-slice_fusion.64
  161.6 71.4 %all-to-all-done.1 = bf16[32,64,1024]{2,1,0:T(8,128)(2,1)} async-done(((bf16[32,64,1024]{2,1,0:T(8,128)(2,1)}), bf16[32,64,1024]{2,1,0:T(8,128)(2,1)}, u32[]{:S(2)}, u32[]{:S(2)}) %all-to-all-start.1) | async-done | bytes 4194336 | tf_op jit(solution)/shard_map/all_to_all | solution.py:53
  233.0 7.3 %all-to-all-start.2 = ((bf16[32,64,1024]{2,1,0:T(8,128)(2,1)}), bf16[32,64,1024]{2,1,0:T(8,128)(2,1)}, u32[]{:S(2)}, u32[]{:S(2)}) async-start(bf16[32,64,1024]{2,1,0:T(8,128)(2,1)} %bitcast.13), calls=%async_computation.2 | async-start | bytes 8388608 | tf_op jit(solution)/shard_map/all_to_all | solution.py:53
  240.4 0.7 all-gather.2.cloned.1.call-update
  241.1 94.5 %all-to-all-done.2 = bf16[32,64,1024]{2,1,0:T(8,128)(2,1)} async-done(((bf16[32,64,1024]{2,1,0:T(8,128)(2,1)}), bf16[32,64,1024]{2,1,0:T(8,128)(2,1)}, u32[]{:S(2)}, u32[]{:S(2)}) %all-to-all-start.2) | async-done | bytes 4194336 | tf_op jit(solution)/shard_map/all_to_all | solution.py:53
  335.6 6.8 %all-to-all-start = ((bf16[32,64,1024]{2,1,0:T(8,128)(2,1)}), bf16[32,64,1024]{2,1,0:T(8,128)(2,1)}, u32[]{:S(2)}, u32[]{:S(2)}) async-start(bf16[32,64,1024]{2,1,0:T(8,128)(2,1)} %bitcast.1), calls=%async_computation | async-start | bytes 8388608 | tf_op jit(solution)/shard_map/all_to_all | solution.py:53
  343.2 2.6 fusion
  345.8 6.8 %fusion.20 = (f32[768]{0:T(1024)S(1)}, f32[768,928]{0,1:T(8,128)S(1)}) fusion(bf16[2048,928]{1,0:T(8,128)(2,1)} %bitcast.8, bf16[768,2048]{1,0:T(8,128)(2,1)} %all-gather.2.cloned.1.call-done, f32[2048]{0:T(1024)S(1)} %convert_element_type.10, f32[768]{0:T(1024)S(1)} %add_rsqrt_fusion), kind=kOutput, calls=%fused_computation.176 | convolution fusion | flops 2926238976 | bytes 9811968 | tf_op jit(solution)/shard_map/dot_general | solution.py:22
  352.7 0.9 multiply_reduce_fusion.3
  353.6 7.4 %fusion.22 = (f32[768]{0:T(1024)S(1)}, f32[768,1024]{1,0:T(8,128)}) fusion(bf16[2048,1024]{1,0:T(8,128)(2,1)} %bitcast.6, bf16[768,2048]{1,0:T(8,128)(2,1)S(1)} %copy-done.4, f32[2048]{0:T(1024)S(1)} %convert_element_type.10, f32[768]{0:T(1024)S(1)} %add_rsqrt_fusion), kind=kOutput, calls=%fused_computation.178 | convolution fusion | flops 3228302592 | bytes 10500096 | tf_op jit(solution)/shard_map/dot_general | solution.py:22
  360.9 7.4 %fusion.21 = (f32[768]{0:T(1024)S(1)}, f32[768,1024]{1,0:T(8,128)}) fusion(bf16[2048,1024]{1,0:T(8,128)(2,1)} %bitcast.4, bf16[768,2048]{1,0:T(8,128)(2,1)S(1)} %copy-done.4, f32[2048]{0:T(1024)S(1)} %convert_element_type.10, f32[768]{0:T(1024)S(1)} %add_rsqrt_fusion), kind=kOutput, calls=%fused_computation.177 | convolution fusion | flops 3228302592 | bytes 10500096 | tf_op jit(solution)/shard_map/dot_general | solution.py:22
  368.3 67.7 %all-to-all-done = bf16[32,64,1024]{2,1,0:T(8,128)(2,1)} async-done(((bf16[32,64,1024]{2,1,0:T(8,128)(2,1)}), bf16[32,64,1024]{2,1,0:T(8,128)(2,1)}, u32[]{:S(2)}, u32[]{:S(2)}) %all-to-all-start) | async-done | bytes 4194336 | tf_op jit(solution)/shard_map/all_to_all | solution.py:53
  436.0 6.6 %fusion.23 = (f32[768]{0:T(1024)S(1)}, f32[768,1024]{1,0:T(8,128)S(1)}) fusion(bf16[2048,1024]{1,0:T(8,128)(2,1)} %bitcast.2, bf16[768,2048]{1,0:T(8,128)(2,1)} %all-gather.2.cloned.1.call-done, f32[2048]{0:T(1024)S(1)} %convert_element_type.10, f32[768]{0:T(1024)S(1)} %add_rsqrt_fusion), kind=kOutput, calls=%fused_computation.179 | convolution fusion | flops 3228302592 | bytes 10500096 | tf_op jit(solution)/shard_map/dot_general | solution.py:22
  442.6 4.4 multiply_reduce_fusion.1
  447.0 14.7 %pmax.7 = f32[768]{0:T(1024)S(1)} all-reduce(f32[768]{0:T(1024)S(1)} %maximum_maximum_fusion), channel_id=1, replica_groups=mesh['dp'=32,'vocab'=8] {'vocab'}, use_global_device_ids=true, to_apply=%region_11.12 | all-reduce | flops 768 | bytes 6144 | tf_op jit(solution)/shard_map/pmax | solution.py:61
  461.9 23.6 %all-reduce = (f32[768]{0:T(1024)S(1)}, f32[768]{0:T(1024)S(1)}, f32[768]{0:T(1024)S(1)}) all-reduce(f32[768]{0:T(1024)S(1)} %add_add_fusion, f32[768]{0:T(1024)S(1)} %get-tuple-element.27, f32[768]{0:T(1024)S(1)} %get-tuple-element.26), channel_id=1, replica_groups=mesh['dp'=32,'vocab'=8] {'vocab'}, use_global_device_ids=true, to_apply=%region_6.7 | all-reduce | flops 2304 | bytes 18432 | tf_op jit(solution)/shard_map/psum | solution.py:63
  485.4 1.2 subtract_select_fusion
  (123 shorter events, 43.7 us)
Async XLA Ops:
  7.2 14.8 %copy-start = (bf16[64,4000]{1,0:T(8,128)(2,1)S(1)}, bf16[64,4000]{1,0:T(8,128)(2,1)}, u32[]{:S(2)}) copy-start(bf16[64,4000]{1,0:T(8,128)(2,1)} %param.8) | copy-start | bytes 1536004
  22.3 2.0 copy-start.1
  24.2 106.9 %all-to-all-start.3 = ((bf16[32,64,928]{2,1,0:T(8,128)(2,1)}), bf16[32,64,928]{2,1,0:T(8,128)(2,1)}, u32[]{:S(2)}, u32[]{:S(2)}) async-start(bf16[32,64,928]{2,1,0:T(8,128)(2,1)} %bitcast.14), calls=%async_computation.3 | async-start | bytes 8388608 | tf_op jit(solution)/shard_map/all_to_all | solution.py:53
  131.2 101.8 %all-to-all-start.1 = ((bf16[32,64,1024]{2,1,0:T(8,128)(2,1)}), bf16[32,64,1024]{2,1,0:T(8,128)(2,1)}, u32[]{:S(2)}, u32[]{:S(2)}) async-start(bf16[32,64,1024]{2,1,0:T(8,128)(2,1)} %bitcast.3), calls=%async_computation.1 | async-start | bytes 8388608 | tf_op jit(solution)/shard_map/all_to_all | solution.py:53
  233.0 102.6 %all-to-all-start.2 = ((bf16[32,64,1024]{2,1,0:T(8,128)(2,1)}), bf16[32,64,1024]{2,1,0:T(8,128)(2,1)}, u32[]{:S(2)}, u32[]{:S(2)}) async-start(bf16[32,64,1024]{2,1,0:T(8,128)(2,1)} %bitcast.13), calls=%async_computation.2 | async-start | bytes 8388608 | tf_op jit(solution)/shard_map/all_to_all | solution.py:53
  240.3 102.9 %all-gather.2.cloned.1.call-start = ((), (), s32[]{:S(2)}) async-start(), calls=%async_computation.4 | async-start | bytes 3538944 | tf_op jit(solution)/shard_map/all_gather | solution.py:41
  335.6 6.8 %copy-start.5 = (bf16[2048]{0:T(1024)(128)(2,1)S(1)}, bf16[2048]{0:T(1024)(128)(2,1)}, u32[]{:S(2)}) copy-start(bf16[2048]{0:T(1024)(128)(2,1)} %param.7) | copy-start | bytes 12292
  335.6 6.9 %copy-start.7 = (s32[64]{0:T(128)S(1)}, s32[64]{0:T(128)}, u32[]{:S(2)}) copy-start(s32[64]{0:T(128)} %param.10) | copy-start | bytes 772
  335.6 6.9 %copy-start.8 = (s32[64]{0:T(128)S(1)}, s32[64]{0:T(128)}, u32[]{:S(2)}) copy-start(s32[64]{0:T(128)} %param.11) | copy-start | bytes 772
  335.6 7.6 %copy-start.6 = (s32[768]{0:T(1024)S(1)}, s32[768]{0:T(1024)}, u32[]{:S(2)}) copy-start(s32[768]{0:T(1024)} %param.9) | copy-start | bytes 9220
  335.6 100.4 %all-to-all-start = ((bf16[32,64,1024]{2,1,0:T(8,128)(2,1)}), bf16[32,64,1024]{2,1,0:T(8,128)(2,1)}, u32[]{:S(2)}, u32[]{:S(2)}) async-start(bf16[32,64,1024]{2,1,0:T(8,128)(2,1)} %bitcast.1), calls=%async_computation | async-start | bytes 8388608 | tf_op jit(solution)/shard_map/all_to_all | solution.py:53
  345.8 7.7 %copy-start.4 = (bf16[768,2048]{1,0:T(8,128)(2,1)S(1)}, bf16[768,2048]{1,0:T(8,128)(2,1)}, u32[]{:S(2)}) copy-start(bf16[768,2048]{1,0:T(8,128)(2,1)} %all-gather.2.cloned.1.call-done) | copy-start | bytes 9437188
  436.0 6.6 %copy-start.2 = (f32[768,1024]{1,0:T(8,128)S(1)}, f32[768,1024]{1,0:T(8,128)}, u32[]{:S(2)}) copy-start(f32[768,1024]{1,0:T(8,128)} %get-tuple-element.39) | copy-start | bytes 9437188
  436.0 6.6 %copy-start.3 = (f32[768,1024]{1,0:T(8,128)S(1)}, f32[768,1024]{1,0:T(8,128)}, u32[]{:S(2)}) copy-start(f32[768,1024]{1,0:T(8,128)} %get-tuple-element.37) | copy-start | bytes 9437188
Sparse Core Ops, SparseCore 0:
  243.0 35.1 all-gather.1
